TPU v7x, 32 devices: a whole 2x2x4 slice. The times are simulated.
32 devices in a mesh: seq: 8 (over z, x), exp: 4 (over y, core).
Axes of the slice: x: 2, y: 2, z: 4, core: 2. Of those that a mesh axis runs over, the one named last changes fastest.
Arguments:
- residual: bfloat16 [4096, 8192], P('seq', 'exp'), may hold values from -16 to 16
- queries: bfloat16 [4096, 4096], P('seq', 'exp'), may hold values from -6 to 6
- keys: bfloat16 [4096, 4096], P('seq', 'exp'), may hold values from -10 to 10
- values: bfloat16 [4096, 4096], P('seq', 'exp'), may hold values from -6 to 6
- documents: int32 [4096], replicated, may hold values from 0 to 1, as said below
- out_proj: bfloat16 [4096, 8192], P(None, 'exp'), may hold values from -0.09375 to 0.09375
- modality: int32 [4096], P('seq'), may hold values from 0 to 1, as said below
- norm_gain: float32 [2, 8192], P(None, 'exp'), may hold values from 0.25 to 1.75
- picks: int32 [4, 64], replicated, may hold values from 0 to 4095, as said below
- router: bfloat16 [8192, 4], P(None, 'exp'), may hold values from -0.0625 to 0.0625
- w_gate: bfloat16 [4, 8192, 4096], P('exp', None, 'seq'), may hold values from -0.0625 to 0.0625
- w_up: bfloat16 [4, 8192, 4096], P('exp', None, 'seq'), may hold values from -0.0625 to 0.0625
- w_down: bfloat16 [4, 4096, 8192], P('exp', 'seq'), may hold values from -0.09375 to 0.09375
Outputs:
- layer_out: bfloat16 [4096, 8192], P('seq', 'exp')
Inputs may be any that keep to these rules, and one draw needn't show every extreme that they name: `modality`: 0 marks a text token, 1 an image token. `documents`: 0 for the first document, 1 for the second; the second begins between position 1024 and 3072. `picks`: row e lists 64 different positions in ascending order; all carry modality 0 for e < 2 and modality 1 otherwise. Within each aligned block of 512 positions (the tokens of one index of seq) a row lists at most 16 positions, and every row lists exactly 16 in some block.
All inputs are finite; a program needn't handle non-finite values.
Results may differ from a plain program's by a relative error of at most 0.0035.
Values may be sent and summed in bfloat16 or wider, within the bound.
A program may use at most 128 MiB of HBM per device.

v0:
```python
import math
import jax
import jax.numpy as jnp
from jax import lax
from jax.sharding import PartitionSpec as P

D = 8192
HD = 128
block_rows = 512


def shards(
    residual,
    queries,
    keys,
    values,
    documents,
    out_proj,
    modality,
    norm_gain,
    picks,
    router,
    w_gate,
    w_up,
    w_down,
):
    tokens = queries.shape[0]
    heads_here = queries.shape[1] // HD
    seq_pos = lax.axis_index("seq")
    start_row = seq_pos * tokens
    query_pos = start_row + jnp.arange(tokens, dtype=jnp.int32)
    query_doc = lax.dynamic_slice_in_dim(documents, start_row, tokens, 0)
    query_heads = queries.reshape(tokens, heads_here, HD)
    score_scale = 1.0 / math.sqrt(HD)

    def attend(state, key_rows, value_rows, key_start):
        row_count = key_rows.shape[0]
        key_pos = key_start + jnp.arange(row_count, dtype=jnp.int32)
        key_doc = lax.dynamic_slice_in_dim(documents, key_start, row_count, 0)
        scores = (
            jnp.einsum(
                "qhd,khd->qhk",
                query_heads,
                key_rows.reshape(row_count, heads_here, HD),
                preferred_element_type=jnp.float32,
            )
            * score_scale
        )
        allowed = (key_pos[None, :] <= query_pos[:, None]) & (
            key_doc[None, :] == query_doc[:, None]
        )
        scores = jnp.where(allowed[:, None, :], scores, -jnp.inf)
        running_max, running_sum, running_out = state
        new_max = jnp.maximum(running_max, jnp.max(scores, axis=2))
        factor = jnp.exp(running_max - new_max)
        weights = jnp.exp(scores - new_max[:, :, None])
        running_sum = running_sum * factor + jnp.sum(weights, axis=2)
        running_out = running_out * factor[:, :, None] + jnp.einsum(
            "qhk,khd->qhd",
            weights.astype(jnp.bfloat16),
            value_rows.reshape(row_count, heads_here, HD),
            preferred_element_type=jnp.float32,
        )
        return (new_max, running_sum, running_out)

    def visit_block(state, key_rows, value_rows, key_start):
        row_count = key_rows.shape[0]
        last_doc = lax.dynamic_index_in_dim(documents, key_start + row_count - 1, 0, keepdims=False)
        beyond = (key_start > query_pos[tokens - 1]) | (last_doc < query_doc[0])
        return lax.cond(
            beyond,
            lambda inner_state: inner_state,
            lambda inner_state: attend(inner_state, key_rows, value_rows, key_start),
            state,
        )

    initial = (
        jnp.full((tokens, heads_here), -1e30, jnp.float32),
        jnp.zeros((tokens, heads_here), jnp.float32),
        jnp.zeros((tokens, heads_here, HD), jnp.float32),
    )
    state = initial
    key_piece = lax.all_gather(keys, "seq", axis=0, tiled=True)
    value_piece = lax.all_gather(values, "seq", axis=0, tiled=True)
    row_count = key_piece.shape[0]
    blocks = row_count // block_rows
    key_stack = key_piece.reshape(blocks, block_rows, key_piece.shape[1])
    value_stack = value_piece.reshape(blocks, block_rows, value_piece.shape[1])

    def scan_step(inner_state, block_item):
        block_index, key_rows, value_rows = block_item
        return (visit_block(inner_state, key_rows, value_rows, block_index * block_rows), None)

    state, unused = lax.scan(
        scan_step, state, (jnp.arange(blocks, dtype=jnp.int32), key_stack, value_stack)
    )
    running_max, running_sum, running_out = state
    attended = (
        (running_out / running_sum[:, :, None])
        .reshape(tokens, heads_here * HD)
        .astype(jnp.bfloat16)
    )
    mixed = jnp.dot(
        lax.all_gather(attended, "exp", axis=1, tiled=True),
        out_proj,
        preferred_element_type=jnp.float32,
    )
    hidden_state = (residual.astype(jnp.float32) + mixed).astype(jnp.bfloat16)
    hidden_wide = hidden_state.astype(jnp.float32)
    square_total = lax.psum(jnp.sum(hidden_wide * hidden_wide, axis=1), "exp")
    inverse = lax.rsqrt(square_total / D + 1e-05)
    gain_rows = jnp.where(modality[:, None] == 0, norm_gain[0][None, :], norm_gain[1][None, :])
    normed = (hidden_wide * inverse[:, None] * gain_rows).astype(jnp.bfloat16)
    capacity = tokens // 32
    inside = (picks >= start_row) & (picks < start_row + tokens)
    slot_index = jnp.cumsum(inside.astype(jnp.int32), axis=1) - 1
    matched = inside[:, None, :] & (
        slot_index[:, None, :] == jnp.arange(capacity, dtype=jnp.int32)[None, :, None]
    )
    local_index = jnp.sum(jnp.where(matched, picks[:, None, :] - start_row, 0), axis=2)
    filled = jnp.any(matched, axis=2)
    rows_out = jnp.take(normed, local_index.T, axis=0)
    rows_out = jnp.where(filled.T[:, :, None], rows_out, jnp.zeros_like(rows_out))
    arrived = lax.all_to_all(rows_out, "exp", split_axis=1, concat_axis=1, tiled=True)
    expert_rows = arrived.reshape(capacity, D)
    logits = jnp.dot(expert_rows, router, preferred_element_type=jnp.float32)[:, 0]
    piece = lax.all_gather(expert_rows, "seq", axis=0, tiled=True)
    gate_part = jnp.dot(piece, w_gate[0], preferred_element_type=jnp.float32)
    up_part = jnp.dot(piece, w_up[0], preferred_element_type=jnp.float32)
    inner_act = (jax.nn.silu(gate_part) * up_part).astype(jnp.bfloat16)
    summed = lax.psum_scatter(
        jnp.dot(inner_act, w_down[0], preferred_element_type=jnp.float32).astype(jnp.bfloat16),
        "seq",
        scatter_dimension=0,
        tiled=True,
    ).astype(jnp.float32)
    weighted = (jax.nn.sigmoid(logits)[:, None] * summed).astype(jnp.bfloat16)
    own_expert = lax.axis_index("exp")
    own_index = lax.dynamic_index_in_dim(local_index, own_expert, 0, keepdims=False)
    own_filled = lax.dynamic_index_in_dim(filled, own_expert, 0, keepdims=False)
    placing = (
        (jnp.arange(tokens, dtype=jnp.int32)[:, None] == own_index[None, :]) & own_filled[None, :]
    ).astype(jnp.bfloat16)
    spread = jnp.dot(placing, weighted, preferred_element_type=jnp.float32)
    expert_add = lax.psum_scatter(
        spread.astype(jnp.bfloat16), "exp", scatter_dimension=1, tiled=True
    ).astype(jnp.float32)
    return (hidden_wide + expert_add).astype(jnp.bfloat16)


def solution(mesh):
    return jax.shard_map(
        shards,
        mesh=mesh,
        in_specs=(
            P("seq", "exp"),
            P("seq", "exp"),
            P("seq", "exp"),
            P("seq", "exp"),
            P(),
            P(None, "exp"),
            P("seq"),
            P(None, "exp"),
            P(),
            P(None, "exp"),
            P("exp", None, "seq"),
            P("exp", None, "seq"),
            P("exp", "seq", None),
        ),
        out_specs=P("seq", "exp"),
        check_vma=False,
    )
```

profile of v0, /device:TPU:0, one launch (start us, length us, event | category | flops | bytes accessed | tf_op | source)
XLA Modules:
  0.0 667.6 jit_solution(14505423510101249050)
XLA Ops:
  6.5 0.7 all-gather.5.cloned.1.call-update
  7.3 0.7 all-gather.7.cloned.1.call-update
  8.1 1.5 copy.56
  9.6 0.7 copy.58
  10.2 0.8 dynamic_slice.55
  11.0 125.7 %all-gather.5.cloned.1.call-done = bf16[4096,1024]{1,0:T(8,128)(2,1)} async-done(((bf16[512,1024]{1,0:T(8,128)(2,1)}), bf16[4096,1024]{1,0:T(8,128)(2,1)}) %all-gather.5.cloned.1.call-update) | async-done | bytes 8388624 | tf_op jit(solution)/shard_map/all_gather | solution.py:83
  136.7 11.6 %copy.57 = bf16[8,512,1024]{1,2,0:T(8,128)(2,1)} copy(bf16[8,512,1024]{2,1,0:T(8,128)(2,1)} %bitcast.77) | data formatting | bytes 16777216 | tf_op jit(solution)/shard_map/while | solution.py:94
  148.3 113.2 %all-gather.7.cloned.1.call-done = bf16[4096,1024]{1,0:T(8,128)(2,1)} async-done(((bf16[512,1024]{1,0:T(8,128)(2,1)}), bf16[4096,1024]{1,0:T(8,128)(2,1)}) %all-gather.7.cloned.1.call-update) | async-done | bytes 8388624 | tf_op jit(solution)/shard_map/all_gather | solution.py:84
  261.5 11.4 %copy.59 = bf16[8,512,1024]{1,2,0:T(8,128)(2,1)} copy(bf16[8,512,1024]{2,1,0:T(8,128)(2,1)} %bitcast.78) | data formatting | bytes 16777216 | tf_op jit(solution)/shard_map/while | solution.py:94
  273.1 55.4 %while.18 = (s32[]{:T(128)}, f32[512,8]{0,1:T(8,128)S(1)}, f32[512,8]{0,1:T(8,128)S(1)}, f32[512,8,128]{2,0,1:T(8,128)S(1)}, s32[8]{0:T(128)S(1)}, /*index=5*/s3...) while((s32[]{:T(128)}, f32[512,8]{0,1:T(8,128)S(1)}, ...), condition=%wide.region_5.6_spmd, body=%wide.region_0.5_spmd.sunk | while | flops 1098654208 | bytes 38025672 | solution.py:94
  273.1 0.6 dynamic_slice.64
  274.4 1.3 dynamic_slice.65
  278.7 9.6 %conditional.2 = (f32[512,8]{0,1:T(8,128)S(1)}, f32[512,8]{0,1:T(8,128)S(1)}, f32[512,8,128]{2,0,1:T(8,128)S(1)}) conditional(s32[]{:T(128)} %convert_element_type.103, (s32[]{:T(128)}, s32[512]{0:T(512)S(1)}, s32[4096]{0:T(1024)}, s32[512]{0:T(512)S(1)}, bf16[8,512,1024]{1,2,0:T(8,128)(2,1)}, /*index=5*/s32[]{:T(128)}, ...), branch_computations={%region_1.3_spmd, %region_4.4_spmd} | conditional | flops 1098654208 | bytes 37992520 | solution.py:70
  278.8 0.8 dynamic_slice.47
  279.8 1.7 constant_dynamic-slice_fusion
  281.5 1.7 fusion.2
  283.2 1.7 fusion.1
  285.0 3.4 bitcast_add_fusion
  288.4 0.6 dynamic_slice.64
  289.6 1.3 dynamic_slice.65
  294.1 0.6 dynamic_slice.64
  295.4 1.3 dynamic_slice.65
  299.8 0.6 dynamic_slice.64
  301.1 1.3 dynamic_slice.65
  305.6 0.6 dynamic_slice.64
  306.8 1.3 dynamic_slice.65
  311.3 0.6 dynamic_slice.64
  312.6 1.3 dynamic_slice.65
  317.0 0.6 dynamic_slice.64
  318.3 1.3 dynamic_slice.65
  322.8 0.6 dynamic_slice.64
  324.0 1.3 dynamic_slice.65
  328.5 1.8 copy.60
  330.3 2.8 divide_convert_fusion
  334.3 79.5 %all-gather.9.cloned.1.call-done = bf16[512,4096]{0,1:T(8,128)(2,1)} async-done(((bf16[512,1024]{0,1:T(8,128)(2,1)}), bf16[512,4096]{0,1:T(8,128)(2,1)}) %all-gather.9.cloned.1.call-update) | async-done | bytes 4194320 | tf_op jit(solution)/shard_map/all_gather | solution.py:104
  413.8 14.2 %fusion.18 = (f32[512]{0:T(512)S(1)}, bf16[512,2048]{1,0:T(8,128)(2,1)S(1)}) fusion(bf16[512,4096]{0,1:T(8,128)(2,1)} %all-gather.9.cloned.1.call-done, bf16[4096,2048]{1,0:T(8,128)(2,1)} %param.22, bf16[512,2048]{1,0:T(8,128)(2,1)} %param.17), kind=kOutput, calls=%fused_computation.30 | convolution fusion | flops 8596226048 | bytes 25167872 | tf_op jit(solution)/shard_map/dot_general | solution.py:103
  428.0 5.9 psum.7
  433.9 2.1 fusion.20
  436.0 2.8 gather_fusion
  439.3 8.7 %all_to_all.5 = bf16[16,4,2048]{2,0,1:T(8,128)(2,1)S(1)} all-to-all(bf16[16,4,2048]{2,0,1:T(8,128)(2,1)S(1)} %fusion.34), channel_id=1, replica_groups=mesh['seq'=8,'exp'=4] {'exp'}, dimensions={1} | all-to-all | bytes 524288 | tf_op jit(solution)/shard_map/all_to_all | solution.py:124
  448.0 0.7 copy.67
  448.8 49.2 %all-gather.11.cloned.1.call-done = bf16[128,8192]{1,0:T(8,128)(2,1)} async-done(((bf16[16,8192]{1,0:T(8,128)(2,1)}), bf16[128,8192]{1,0:T(8,128)(2,1)}) %all-gather.11.cloned.1.call-update) | async-done | bytes 2097168 | tf_op jit(solution)/shard_map/all_gather | solution.py:127
  498.0 5.4 fusion.16
  503.5 9.6 %convolution_convert_fusion.1 = bf16[128,8192]{1,0:T(8,128)(2,1)} fusion(bf16[1,512,8192]{2,1,0:T(8,128)(2,1)} %param.29, bf16[128,8192]{1,0:T(8,128)(2,1)S(1)} %copy-done.1, bf16[1,8192,512]{2,1,0:T(8,128)(2,1)} %param.28, f32[128,512]{1,0:T(8,128)S(1)} %fusion.16), kind=kOutput, calls=%fused_computation.21 | convolution fusion | flops 2148925440 | bytes 21233664 | tf_op jit(solution)/shard_map/dot_general | solution.py:132
  513.6 66.4 %reduce-scatter.3.cloned.1.call-done = bf16[16,8192]{1,0:T(8,128)(2,1)} async-done(((bf16[128,8192]{1,0:T(8,128)(2,1)}), bf16[16,8192]{1,0:T(8,128)(2,1)}) %reduce-scatter.3.cloned.1.call-update) | async-done | bytes 262160 | tf_op jit(solution)/shard_map/reduce_scatter | solution.py:131
  580.1 6.6 convolution_convert_fusion
  586.7 70.4 %reduce-scatter.5.cloned.1.call-done = bf16[512,2048]{1,0:T(8,128)(2,1)} async-done(((bf16[512,8192]{1,0:T(8,128)(2,1)}), bf16[512,2048]{1,0:T(8,128)(2,1)}) %reduce-scatter.5.cloned.1.call-update) | async-done | bytes 2097168 | tf_op jit(solution)/shard_map/reduce_scatter | solution.py:145
  657.1 3.7 fusion.21
  (91 shorter events, 12.3 us)
Async XLA Ops:
  6.5 506.9 %copy-start = (bf16[8192,1]{0,1:T(2,128)(2,1)S(1)}, bf16[8192,1]{0,1:T(2,128)(2,1)}, u32[]{:S(2)}) copy-start(bf16[8192,1]{0,1:T(2,128)(2,1)} %param.26) | copy-start | bytes 49156
  6.5 130.1 %all-gather.5.cloned.1.call-start = ((), (), s32[]{:S(2)}) async-start(), calls=%async_computation.3 | async-start | bytes 9437184 | tf_op jit(solution)/shard_map/all_gather | solution.py:83
  7.3 254.2 %all-gather.7.cloned.1.call-start = ((), (), s32[]{:S(2)}) async-start(), calls=%async_computation.4 | async-start | bytes 9437184 | tf_op jit(solution)/shard_map/all_gather | solution.py:84
  8.0 405.8 %all-gather.9.cloned.1.call-start = ((), (), s32[]{:S(2)}) async-start(), calls=%async_computation.5 | async-start | bytes 5242880 | tf_op jit(solution)/shard_map/all_gather | solution.py:104
  328.5 4.9 copy-start.6
  328.5 5.7 copy-start.7
  328.5 5.7 copy-start.5
  333.2 164.8 %all-gather.11.cloned.1.call-start = ((), (), s32[]{:S(2)}) async-start(), calls=%async_computation.6 | async-start | bytes 2359296 | tf_op jit(solution)/shard_map/all_gather | solution.py:127
  428.0 20.8 %copy-start.2 = (bf16[512,2048]{1,0:T(8,128)(2,1)}, bf16[512,2048]{1,0:T(8,128)(2,1)S(1)}, u32[]{:S(2)}) copy-start(bf16[512,2048]{1,0:T(8,128)(2,1)S(1)} %get-tuple-element.425) | copy-start | bytes 6291460
  448.8 131.3 %reduce-scatter.3.cloned.1.call-start = ((), (), s32[]{:S(2)}) async-start(), calls=%async_computation.7 | async-start | bytes 2359296 | tf_op jit(solution)/shard_map/reduce_scatter | solution.py:131
  498.0 5.4 copy-start.1
  503.5 10.0 %copy-start.4 = (bf16[4,2,8,2048]{3,2,0,1:T(8,128)(2,1)S(1)}, bf16[4,2,8,2048]{3,2,0,1:T(8,128)(2,1)}, u32[]{:S(2)}) copy-start(bf16[4,2,8,2048]{3,2,0,1:T(8,128)(2,1)} %copy.67) | copy-start | bytes 786436
  513.1 144.0 %reduce-scatter.5.cloned.1.call-start = ((), (), s32[]{:S(2)}) async-start(), calls=%async_computation.8 | async-start | bytes 10485760 | tf_op jit(solution)/shard_map/reduce_scatter | solution.py:145
  586.6 70.5 %copy-start.3 = (bf16[512,2048]{1,0:T(8,128)(2,1)S(1)}, bf16[512,2048]{1,0:T(8,128)(2,1)}, u32[]{:S(2)}) copy-start(bf16[512,2048]{1,0:T(8,128)(2,1)} %copy-done.2) | copy-start | bytes 6291460
Sparse Core Ops, SparseCore 0:
  9.5 127.1 all-gather.4
  138.8 122.6 all-gather.6
  333.3 80.4 all-gather.8
  448.9 49.0 all-gather.10
  513.2 66.7 reduce-scatter.2
  586.8 70.2 reduce-scatter.4
where the time goes:
time: 669 us; the launch traced here: 668 us
  waiting for transfers between devices  506 us (76%)
  local copies, waits for them, and re-layouts  59.3 us (9%)
  matrix products  41 us (6%)
  loops' own time  20.9 us (3%)
  blocking collectives  14.6 us (2%)
  between operations  13.7 us (2%)
  other arithmetic  11.6 us (2%)
    all_gather x1, waiting for transfers between devices, shards(): key_piece = lax.all_gather(keys, 'seq', axis=0, tiled=True)  126 us
    all_gather x1, waiting for transfers between devices, shards(): value_piece = lax.all_gather(values, 'seq', axis=0, tiled=True)  113 us
    all_gather x1, waiting for transfers between devices, shards(): lax.all_gather(attended, 'exp', axis=1, tiled=True)  79.5 us
    reduce_scatter x1, waiting for transfers between devices, shards(): lax.psum_scatter(spread.astype(jnp.bfloat16), 'exp', scatter_dimension=1,...  70.4 us
    reduce_scatter x1, waiting for transfers between devices, shards(): lax.psum_scatter(jnp.dot(inner_act, w_down[0], preferred_element_type=jnp...  66.4 us
    all_gather x1, waiting for transfers between devices, shards(): piece = lax.all_gather(expert_rows, 'seq', axis=0, tiled=True)  49.2 us
    while x4, local copies, waits for them, and re-layouts, shards(): lax.scan(scan_step, state, (jnp.arange(blocks, dtype=jnp.int32), key_stac...  25.5 us
    another operation x1, loops' own time, shards(): lax.scan(scan_step, state, (jnp.arange(blocks, dtype=jnp.int32), key_stac...  20.7 us
  transfers between devices with their start and end apart: 6, of which 6 were waited for; matrix products, arithmetic and copies ran while one was open for 2% of the time, Pallas kernels for 0%

commit v1 on v0

--- a/solution.py
+++ b/solution.py
@@ -7,6 +7,9 @@
 D = 8192
 HD = 128
 block_rows = 512
+page_show = lambda dim_k, local_block: jnp.concatenate(
+    lax.all_gather(local_block, axis_name="exp"), dim_k
+)
 
 
 def shards(
@@ -100,11 +103,7 @@
         .reshape(tokens, heads_here * HD)
         .astype(jnp.bfloat16)
     )
-    mixed = jnp.dot(
-        lax.all_gather(attended, "exp", axis=1, tiled=True),
-        out_proj,
-        preferred_element_type=jnp.float32,
-    )
+    mixed = jnp.dot(page_show(1, attended), out_proj, preferred_element_type=jnp.float32)
     hidden_state = (residual.astype(jnp.float32) + mixed).astype(jnp.bfloat16)
     hidden_wide = hidden_state.astype(jnp.float32)
     square_total = lax.psum(jnp.sum(hidden_wide * hidden_wide, axis=1), "exp")

time: 669 us -> 676 us (1.010)
  local copies, waits for them, and re-layouts: 59.3 us -> 66.9 us
where the time goes in v1:
time: 676 us; the launch traced here: 675 us
  waiting for transfers between devices  506 us (75%)
  local copies, waits for them, and re-layouts  66.9 us (10%)
  matrix products  41 us (6%)
  loops' own time  20.9 us (3%)
  blocking collectives  14.6 us (2%)
  between operations  13.7 us (2%)
  other arithmetic  10.7 us (2%)
    all_gather x1, waiting for transfers between devices, shards(): key_piece = lax.all_gather(keys, 'seq', axis=0, tiled=True)  126 us
    all_gather x1, waiting for transfers between devices, shards(): value_piece = lax.all_gather(values, 'seq', axis=0, tiled=True)  113 us
    all_gather x1, waiting for transfers between devices, lax.all_gather(local_block, axis_name='exp')  79.5 us
    reduce_scatter x1, waiting for transfers between devices, shards(): lax.psum_scatter(spread.astype(jnp.bfloat16), 'exp', scatter_dimension=1,...  70.5 us
    reduce_scatter x1, waiting for transfers between devices, shards(): lax.psum_scatter(jnp.dot(inner_act, w_down[0], preferred_element_type=jnp...  66.7 us
    all_gather x1, waiting for transfers between devices, shards(): piece = lax.all_gather(expert_rows, 'seq', axis=0, tiled=True)  49.2 us
    while x4, local copies, waits for them, and re-layouts, shards(): lax.scan(scan_step, state, (jnp.arange(blocks, dtype=jnp.int32), key_stac...  25.5 us
    another operation x1, loops' own time, shards(): lax.scan(scan_step, state, (jnp.arange(blocks, dtype=jnp.int32), key_stac...  20.7 us
  transfers between devices with their start and end apart: 6, of which 6 were waited for; matrix products, arithmetic and copies ran while one was open for 2% of the time, Pallas kernels for 0%

profile of v1, /device:TPU:0, one launch (start us, length us, event | category | flops | bytes accessed | tf_op | source)
XLA Modules:
  0.0 674.6 jit_solution(9337841595333922027)
XLA Ops:
  6.5 0.7 all-gather.5.cloned.1.call-update
  7.3 0.7 all-gather.7.cloned.1.call-update
  8.1 1.5 copy.60
  9.6 0.7 copy.62
  10.2 0.8 dynamic_slice.55
  11.0 125.7 %all-gather.5.cloned.1.call-done = bf16[4096,1024]{1,0:T(8,128)(2,1)} async-done(((bf16[512,1024]{1,0:T(8,128)(2,1)}), bf16[4096,1024]{1,0:T(8,128)(2,1)}) %all-gather.5.cloned.1.call-update) | async-done | bytes 8388624 | tf_op jit(solution)/shard_map/all_gather | solution.py:86
  136.7 11.6 %copy.61 = bf16[8,512,1024]{1,2,0:T(8,128)(2,1)} copy(bf16[8,512,1024]{2,1,0:T(8,128)(2,1)} %bitcast.80) | data formatting | bytes 16777216 | tf_op jit(solution)/shard_map/while | solution.py:97
  148.3 113.2 %all-gather.7.cloned.1.call-done = bf16[4096,1024]{1,0:T(8,128)(2,1)} async-done(((bf16[512,1024]{1,0:T(8,128)(2,1)}), bf16[4096,1024]{1,0:T(8,128)(2,1)}) %all-gather.7.cloned.1.call-update) | async-done | bytes 8388624 | tf_op jit(solution)/shard_map/all_gather | solution.py:87
  261.5 11.4 %copy.63 = bf16[8,512,1024]{1,2,0:T(8,128)(2,1)} copy(bf16[8,512,1024]{2,1,0:T(8,128)(2,1)} %bitcast.81) | data formatting | bytes 16777216 | tf_op jit(solution)/shard_map/while | solution.py:97
  273.1 55.4 %while.18 = (s32[]{:T(128)}, f32[512,8]{0,1:T(8,128)S(1)}, f32[512,8]{0,1:T(8,128)S(1)}, f32[512,8,128]{2,0,1:T(8,128)S(1)}, s32[8]{0:T(128)S(1)}, /*index=5*/s3...) while((s32[]{:T(128)}, f32[512,8]{0,1:T(8,128)S(1)}, ...), condition=%wide.region_5.6_spmd, body=%wide.region_0.5_spmd.sunk | while | flops 1098654208 | bytes 38025672 | solution.py:97
  273.1 0.6 dynamic_slice.64
  274.4 1.3 dynamic_slice.65
  278.7 9.6 %conditional.2 = (f32[512,8]{0,1:T(8,128)S(1)}, f32[512,8]{0,1:T(8,128)S(1)}, f32[512,8,128]{2,0,1:T(8,128)S(1)}) conditional(s32[]{:T(128)} %convert_element_type.110, (s32[]{:T(128)}, s32[512]{0:T(512)S(1)}, s32[4096]{0:T(1024)}, s32[512]{0:T(512)S(1)}, bf16[8,512,1024]{1,2,0:T(8,128)(2,1)}, /*index=5*/s32[]{:T(128)}, ...), branch_computations={%region_1.3_spmd, %region_4.4_spmd} | conditional | flops 1098654208 | bytes 37992520 | solution.py:73
  278.8 0.8 dynamic_slice.47
  279.8 1.7 constant_dynamic-slice_fusion
  281.5 1.7 fusion.2
  283.2 1.7 fusion.1
  285.0 3.4 bitcast_add_fusion
  288.4 0.6 dynamic_slice.64
  289.6 1.3 dynamic_slice.65
  294.1 0.6 dynamic_slice.64
  295.4 1.3 dynamic_slice.65
  299.8 0.6 dynamic_slice.64
  301.1 1.3 dynamic_slice.65
  306.8 1.3 dynamic_slice.65
  311.3 0.6 dynamic_slice.64
  312.6 1.3 dynamic_slice.65
  317.0 0.6 dynamic_slice.64
  318.3 1.3 dynamic_slice.65
  324.0 1.3 dynamic_slice.65
  328.5 1.8 copy.64
  330.3 1.9 divide_convert_fusion
  332.2 1.3 copy.65
  334.6 79.5 %all-gather.9.cloned.1.call-done = bf16[4,512,1024]{2,1,0:T(8,128)(2,1)} async-done(((bf16[1,512,1024]{2,1,0:T(8,128)(2,1)}), bf16[4,512,1024]{2,1,0:T(8,128)(2,1)}) %all-gather.9.cloned.1.call-update) | async-done | bytes 4194320 | tf_op jit(solution)/shard_map/all_gather | solution.py:11
  414.2 6.3 copy.66
  420.5 14.2 %fusion.18 = (f32[512]{0:T(512)S(1)}, bf16[512,2048]{1,0:T(8,128)(2,1)S(1)}) fusion(bf16[512,4096]{0,1:T(8,128)(2,1)} %bitcast.83, bf16[4096,2048]{1,0:T(8,128)(2,1)} %param.22, bf16[512,2048]{1,0:T(8,128)(2,1)} %param.17), kind=kOutput, calls=%fused_computation.30 | convolution fusion | flops 8596226048 | bytes 25167872 | tf_op jit(solution)/shard_map/dot_general | solution.py:106
  434.6 5.9 psum.7
  440.5 2.1 fusion.20
  442.7 2.8 gather_fusion
  446.0 8.7 %all_to_all.5 = bf16[16,4,2048]{2,0,1:T(8,128)(2,1)S(1)} all-to-all(bf16[16,4,2048]{2,0,1:T(8,128)(2,1)S(1)} %fusion.34), channel_id=1, replica_groups=mesh['seq'=8,'exp'=4] {'exp'}, dimensions={1} | all-to-all | bytes 524288 | tf_op jit(solution)/shard_map/all_to_all | solution.py:123
  454.7 0.7 copy.73
  455.5 49.2 %all-gather.11.cloned.1.call-done = bf16[128,8192]{1,0:T(8,128)(2,1)} async-done(((bf16[16,8192]{1,0:T(8,128)(2,1)}), bf16[128,8192]{1,0:T(8,128)(2,1)}) %all-gather.11.cloned.1.call-update) | async-done | bytes 2097168 | tf_op jit(solution)/shard_map/all_gather | solution.py:126
  504.7 5.4 fusion.16
  510.1 9.6 %convolution_convert_fusion.1 = bf16[128,8192]{1,0:T(8,128)(2,1)} fusion(bf16[1,512,8192]{2,1,0:T(8,128)(2,1)} %param.29, bf16[128,8192]{1,0:T(8,128)(2,1)S(1)} %copy-done.1, bf16[1,8192,512]{2,1,0:T(8,128)(2,1)} %param.28, f32[128,512]{1,0:T(8,128)S(1)} %fusion.16), kind=kOutput, calls=%fused_computation.21 | convolution fusion | flops 2148925440 | bytes 21233664 | tf_op jit(solution)/shard_map/dot_general | solution.py:131
  520.3 66.7 %reduce-scatter.3.cloned.1.call-done = bf16[16,8192]{1,0:T(8,128)(2,1)} async-done(((bf16[128,8192]{1,0:T(8,128)(2,1)}), bf16[16,8192]{1,0:T(8,128)(2,1)}) %reduce-scatter.3.cloned.1.call-update) | async-done | bytes 262160 | tf_op jit(solution)/shard_map/reduce_scatter | solution.py:130
  587.0 6.6 convolution_convert_fusion
  593.6 70.5 %reduce-scatter.5.cloned.1.call-done = bf16[512,2048]{1,0:T(8,128)(2,1)} async-done(((bf16[512,8192]{1,0:T(8,128)(2,1)}), bf16[512,2048]{1,0:T(8,128)(2,1)}) %reduce-scatter.5.cloned.1.call-update) | async-done | bytes 2097168 | tf_op jit(solution)/shard_map/reduce_scatter | solution.py:144
  664.1 3.7 fusion.21
  (93 shorter events, 13.6 us)
Async XLA Ops:
  6.5 513.5 %copy-start = (bf16[8192,1]{0,1:T(2,128)(2,1)S(1)}, bf16[8192,1]{0,1:T(2,128)(2,1)}, u32[]{:S(2)}) copy-start(bf16[8192,1]{0,1:T(2,128)(2,1)} %param.26) | copy-start | bytes 49156
  6.5 130.1 %all-gather.5.cloned.1.call-start = ((), (), s32[]{:S(2)}) async-start(), calls=%async_computation.3 | async-start | bytes 9437184 | tf_op jit(solution)/shard_map/all_gather | solution.py:86
  7.3 254.2 %all-gather.7.cloned.1.call-start = ((), (), s32[]{:S(2)}) async-start(), calls=%async_computation.4 | async-start | bytes 9437184 | tf_op jit(solution)/shard_map/all_gather | solution.py:87
  8.0 406.2 %all-gather.9.cloned.1.call-start = ((), (), s32[]{:S(2)}) async-start(), calls=%async_computation.5 | async-start | bytes 5242880 | tf_op jit(solution)/shard_map/all_gather | solution.py:11
  330.3 3.5 copy-start.6
  330.3 4.3 copy-start.7
  330.3 4.3 copy-start.5
  333.6 171.1 %all-gather.11.cloned.1.call-start = ((), (), s32[]{:S(2)}) async-start(), calls=%async_computation.6 | async-start | bytes 2359296 | tf_op jit(solution)/shard_map/all_gather | solution.py:126
  434.6 20.8 %copy-start.2 = (bf16[512,2048]{1,0:T(8,128)(2,1)}, bf16[512,2048]{1,0:T(8,128)(2,1)S(1)}, u32[]{:S(2)}) copy-start(bf16[512,2048]{1,0:T(8,128)(2,1)S(1)} %get-tuple-element.425) | copy-start | bytes 6291460
  455.4 131.6 %reduce-scatter.3.cloned.1.call-start = ((), (), s32[]{:S(2)}) async-start(), calls=%async_computation.7 | async-start | bytes 2359296 | tf_op jit(solution)/shard_map/reduce_scatter | solution.py:130
  504.7 5.4 copy-start.1
  510.1 10.0 %copy-start.4 = (bf16[4,2,8,2048]{3,2,0,1:T(8,128)(2,1)S(1)}, bf16[4,2,8,2048]{3,2,0,1:T(8,128)(2,1)}, u32[]{:S(2)}) copy-start(bf16[4,2,8,2048]{3,2,0,1:T(8,128)(2,1)} %copy.73) | copy-start | bytes 786436
  519.8 144.3 %reduce-scatter.5.cloned.1.call-start = ((), (), s32[]{:S(2)}) async-start(), calls=%async_computation.8 | async-start | bytes 10485760 | tf_op jit(solution)/shard_map/reduce_scatter | solution.py:144
  593.5 70.5 %copy-start.3 = (bf16[512,2048]{1,0:T(8,128)(2,1)S(1)}, bf16[512,2048]{1,0:T(8,128)(2,1)}, u32[]{:S(2)}) copy-start(bf16[512,2048]{1,0:T(8,128)(2,1)} %copy-done.2) | copy-start | bytes 6291460
Sparse Core Ops, SparseCore 0:
  9.5 127.1 all-gather.4
  138.8 122.6 all-gather.6
  333.7 80.4 all-gather.8
  455.5 49.0 all-gather.10
  519.9 67.0 reduce-scatter.2
  593.7 70.3 reduce-scatter.4
